TPU v7x, 256 devices: a whole 4x4x8 slice. The times are simulated.
256 devices in a mesh: dp: 64 (over x, z, core), dim: 4 (over y).
Axes of the slice: x: 4, y: 4, z: 8, core: 2. Of those that a mesh axis runs over, the one named last changes fastest.
Arguments:
- vectors: bfloat16 [768, 65536], P('dim', 'dp'), may hold values from -30 to 30
- codes: int32 [64, 65536], P('dim', 'dp'), may hold values from 0 to 255, as said below
- codebook: bfloat16 [256, 768], P(None, 'dim'), may hold values from -4 to 4
Outputs:
- rotation: float32 [768, 768], P('dim')
- new_codebook: float32 [256, 768], P('dp', 'dim')
Inputs may be any that keep to these rules, and one draw needn't show every extreme that they name: `codes`: each entry names a centroid of its subspace; in each subspace at least one centroid, which one is drawn from the seed, is named by no vector.
All inputs are finite; a program needn't handle non-finite values.
Results may differ from a plain program's by a relative error of at most 0.003.
Values may be sent and summed in bfloat16 or wider, within the bound.
A program may use at most 64 MiB of HBM per device.

v0:
```python
import jax
import jax.numpy as jnp
from jax import lax
from jax.sharding import PartitionSpec as P

NS_STEPS = 4


def per_device(vectors, codes, codebook):
    local_width = vectors.shape[0]
    row_count = vectors.shape[1]
    sub_local = codes.shape[0]
    sub_width = local_width // sub_local
    centroid_count = codebook.shape[0]
    dp_count = lax.axis_size("dp")
    dim_count = lax.axis_size("dim")
    total_width = local_width * dim_count
    block_rows = min(512, row_count)
    block_count = row_count // block_rows
    levels = jnp.arange(centroid_count, dtype=jnp.int32)
    book_cube = codebook.reshape(centroid_count, sub_local, sub_width)
    gathered_rows = lax.all_gather(vectors, "dim", axis=0, tiled=True)

    def block_onehot(block_index):
        start = block_index * block_rows
        code_block = lax.dynamic_slice_in_dim(codes, start, block_rows, 1)
        onehot = (code_block[:, :, None] == levels[None, None, :]).astype(jnp.bfloat16)
        row_block = lax.dynamic_slice_in_dim(gathered_rows, start, block_rows, 1)
        return (onehot, row_block)

    def add_cross(block_index, cross_part):
        onehot, row_block = block_onehot(block_index)
        decoded = jnp.einsum("mnk,kmd->nmd", onehot, book_cube, preferred_element_type=jnp.float32)
        decoded = decoded.reshape(block_rows, local_width).astype(jnp.bfloat16)
        return cross_part + jnp.einsum(
            "nd,cn->dc", decoded, row_block, preferred_element_type=jnp.float32
        )

    cross_part = lax.fori_loop(
        0, block_count, add_cross, jnp.zeros((local_width, total_width), jnp.float32)
    )

    def newton_update(rows, whole):
        gram_rows = jnp.dot(rows, whole.T, precision=lax.Precision.HIGHEST)
        return 1.5 * rows - 0.5 * jnp.dot(gram_rows, whole, precision=lax.Precision.HIGHEST)

    own_rows = lax.psum_scatter(cross_part, "dp", scatter_dimension=0, tiled=True)
    thin_width = own_rows.shape[0]
    dim_index = lax.axis_index("dim")

    def gather_spread(rows):
        return lax.all_gather(rows, ("dp", "dim"), axis=0, tiled=True)

    gathered = gather_spread(own_rows)
    magnitude = jnp.sqrt(jnp.sum(gathered * gathered))
    gathered = gathered / magnitude
    own_rows = own_rows / magnitude

    def spread_step(iteration, carry):
        rows, whole = carry
        rows = newton_update(rows, whole)
        return (rows, gather_spread(rows))

    own_rows, gathered = lax.fori_loop(0, NS_STEPS - 1, spread_step, (own_rows, gathered))
    shaped = gathered.reshape(dp_count, dim_count, thin_width, total_width)
    block_part = lax.dynamic_slice_in_dim(shaped, dim_index, 1, 1).reshape(local_width, total_width)
    rotation = newton_update(block_part, gathered)
    rotation_low = rotation.astype(jnp.bfloat16)

    def add_centroids(block_index, carry):
        centroid_sums, counts = carry
        onehot, row_block = block_onehot(block_index)
        rotated = jnp.einsum(
            "cn,dc->nd", row_block, rotation_low, preferred_element_type=jnp.float32
        ).astype(jnp.bfloat16)
        rotated = rotated.reshape(block_rows, sub_local, sub_width)
        centroid_sums = centroid_sums + jnp.einsum(
            "mnk,nmd->kmd", onehot, rotated, preferred_element_type=jnp.float32
        )
        counts = counts + jnp.sum(onehot, axis=1, dtype=jnp.float32).T
        return (centroid_sums, counts)

    start_sums = jnp.zeros((centroid_count, sub_local, sub_width), jnp.float32)
    start_counts = jnp.zeros((centroid_count, sub_local), jnp.float32)
    centroid_sums, counts = lax.fori_loop(0, block_count, add_centroids, (start_sums, start_counts))
    owned_sums, owned_counts = (
        lax.psum_scatter(
            centroid_sums.reshape(centroid_count, local_width),
            "dp",
            scatter_dimension=0,
            tiled=True,
        ),
        lax.psum_scatter(counts, "dp", scatter_dimension=0, tiled=True),
    )
    divisor = jnp.repeat(jnp.maximum(owned_counts, 1.0), sub_width, axis=1)
    new_codebook = owned_sums / divisor
    return (rotation, new_codebook)


def solution(mesh):
    placed = (P("dim", "dp"), P("dim", "dp"), P(None, "dim"))
    return jax.shard_map(
        per_device,
        mesh=mesh,
        in_specs=placed,
        out_specs=(P("dim", None), P("dp", "dim")),
        check_vma=False,
    )
```

profile of v0, /device:TPU:8, one launch (start us, length us, event | category | flops | bytes accessed | tf_op | source)
XLA Modules:
  0.0 973.8 jit_solution(7501567277466070156)
XLA Ops:
  7.2 0.0 all-gather.8.cloned.1.call-start
  7.2 0.7 all-gather.8.cloned.1.call-update
  7.9 0.0 all-reduce.6.cloned.1.call-start
  8.0 0.9 reshape.36
  8.9 31.9 %all-gather.8.cloned.1.call-done = bf16[768,1024]{1,0:T(8,128)(2,1)} async-done(((bf16[192,1024]{1,0:T(8,128)(2,1)}), bf16[768,1024]{1,0:T(8,128)(2,1)}) %all-gather.8.cloned.1.call-update) | async-done | bytes 1572880 | tf_op jit(solution)/shard_map/all_gather | solution.py:22
  40.8 6.8 while.43
  40.8 0.8 constant_dynamic-slice_fusion.7
  41.5 2.0 fusion.57
  43.5 0.1 convert_element_type.62
  43.6 0.5 convolution_add_fusion.2
  44.2 0.8 constant_dynamic-slice_fusion.7
  44.9 2.0 fusion.57
  46.9 0.1 convert_element_type.62
  47.0 0.5 convolution_add_fusion.2
  47.6 0.8 copy-done.1
  48.4 0.0 all-gather.10.cloned.1.call-start
  48.5 0.6 dynamic-slice
  49.6 182.2 %all-reduce.6.cloned.1.call-done = f32[192,768]{1,0:T(8,128)} async-done(((f32[192,768]{1,0:T(8,128)}), f32[192,768]{1,0:T(8,128)}) %all-reduce.6.cloned.1.call-update) | async-done | bytes 589840
  231.8 1.4 dynamic-slice_bitcast_fusion
  233.8 106.4 %all-gather.10.cloned.1.call-done = f32[256,3,768]{2,1,0:T(4,128)} async-done(((f32[1,3,768]{2,1,0:T(4,128)}), f32[256,3,768]{2,1,0:T(4,128)}) %all-gather.10.cloned.1.call-update) | async-done | bytes 2359312 | tf_op jit(solution)/shard_map/all_gather | solution.py:52
  340.2 4.3 multiply_reduce_fusion
  345.2 2.2 broadcast_divide_fusion
  347.4 3.2 reshape.47
  350.6 0.8 dynamic-slice_divide_fusion
  351.4 337.2 %while.42 = (s32[]{:T(128)}, f32[3,768]{1,0:T(4,128)S(1)}, f32[768,768]{1,0:T(8,128)S(1)}, s32[]{:T(128)}) while((s32[]{:T(128)}, f32[3,768]{1,0:T(4,128)S(1)}, f32[768,768]{1,0:T(8,128)S(1)}, s32[]{:T(128)}) %tuple.81), condition=%wide.region_5.0_spmd, body=%wide.region_4.0_spmd.sunk | while | flops 42474240 | bytes 17452180 | solution.py:64
  351.5 2.0 fusion.52
  353.5 1.2 fusion.53
  354.7 0.6 copy-done.3
  355.4 105.2 %all-gather.12.cloned.1.call-done = f32[256,3,768]{2,1,0:T(4,128)} async-done(((f32[1,3,768]{2,1,0:T(4,128)}), f32[256,3,768]{2,1,0:T(4,128)}) %all-gather.12.cloned.1.call-update) | async-done | bytes 2359312 | tf_op jit(solution)/shard_map/while/body/eval_jaxpr/all_gather | solution.py:52
  460.6 3.2 reshape.58
  463.9 0.0 all-gather.12.cloned.1.call-start
  463.9 2.0 fusion.52
  465.9 1.2 fusion.53
  467.1 0.6 copy-done.3
  467.8 105.2 %all-gather.12.cloned.1.call-done = f32[256,3,768]{2,1,0:T(4,128)} async-done(((f32[1,3,768]{2,1,0:T(4,128)}), f32[256,3,768]{2,1,0:T(4,128)}) %all-gather.12.cloned.1.call-update) | async-done | bytes 2359312 | tf_op jit(solution)/shard_map/while/body/eval_jaxpr/all_gather | solution.py:52
  573.0 3.2 reshape.58
  576.3 0.0 all-gather.12.cloned.1.call-start
  576.3 2.0 fusion.52
  578.3 1.2 fusion.53
  579.6 0.6 copy-done.3
  580.2 105.2 %all-gather.12.cloned.1.call-done = f32[256,3,768]{2,1,0:T(4,128)} async-done(((f32[1,3,768]{2,1,0:T(4,128)}), f32[256,3,768]{2,1,0:T(4,128)}) %all-gather.12.cloned.1.call-update) | async-done | bytes 2359312 | tf_op jit(solution)/shard_map/while/body/eval_jaxpr/all_gather | solution.py:52
  685.4 3.2 reshape.58
  688.7 0.0 all-reduce.8.cloned.1.call-start
  688.7 2.6 reshape.37
  691.3 2.2 constant_dynamic-slice_fusion.4
  693.5 1.4 reshape.38
  694.9 2.5 fusion.21
  697.4 2.6 fusion.19
  700.0 12.7 %while.44 = (s32[]{:T(128)}, f32[256,16,12]{0,2,1:T(8,128)}, f32[256,16]{0,1:T(8,128)S(1)}, bf16[768,1024]{1,0:T(8,128)(2,1)}, bf16[192,768]{1,0:T(8,128)(2,1)S(...) while((s32[]{:T(128)}, f32[256,16,12]{0,2,1:T(8,128)}, ...), condition=%wide.region_8.0_spmd.clone, body=%wide.region_6.0_spmd.clone.sunk | while | flops 212013056 | bytes 2457774 | solution.py:85
  700.0 1.4 convolution_convert_fusion.2
  701.5 2.8 fusion.61
  704.3 1.4 convert_reduce_fusion.2
  705.8 1.5 convolution_convert_fusion.2
  707.3 3.9 fusion.61
  711.2 1.4 convert_reduce_fusion.2
  712.7 1.7 reshape.39
  714.3 250.5 %all-reduce.2 = f32[256,16]{0,1:T(8,128)S(1)} all-reduce(f32[256,16]{0,1:T(8,128)S(1)} %get-tuple-element.256), channel_id=4, replica_groups=mesh['dp'=64,'dim'=4] {'dp'}, use_global_device_ids=true, to_apply=%region_10.0.clone | all-reduce | flops 4096 | bytes 32768
  964.9 0.1 constant_dynamic-slice_fusion.2
  965.0 0.1 copy.13
  965.0 0.1 broadcast_in_dim.27
  965.1 0.1 reshape.40
  965.2 1.0 constant_dynamic-slice_fusion.3
  966.2 0.1 copy.14
  966.3 0.6 div.19
  (38 shorter events, 0.3 us)
Async XLA Ops:
  7.2 33.6 %all-gather.8.cloned.1.call-start = ((), (), s32[]{:S(2)}) async-start(), calls=%async_computation | async-start | bytes 1966080 | tf_op jit(solution)/shard_map/all_gather | solution.py:22
  7.9 223.9 %all-reduce.6.cloned.1.call-start = ((), (), s32[]{:S(2)}) async-start(), calls=%async_computation.2 | async-start | bytes 1179648
  40.8 7.7 copy-start.6
  41.5 2.1 copy-start
  44.9 2.1 copy-start
  47.5 0.8 copy-start.1
  48.4 291.8 %all-gather.10.cloned.1.call-start = ((), (), s32[]{:S(2)}) async-start(), calls=%async_computation.1 | async-start | bytes 3158016 | tf_op jit(solution)/shard_map/all_gather | solution.py:52
  340.2 5.0 copy-start.2
  351.4 109.1 %all-gather.12.cloned.1.call-start = ((), (), s32[]{:S(2)}) async-start(), calls=%async_computation.4 | async-start | bytes 3158016 | tf_op jit(solution)/shard_map/while/body/eval_jaxpr/all_gather | solution.py:52
  354.7 0.6 copy-start.3
  355.3 108.5 %copy-start.4 = (f32[3,768]{1,0:T(4,128)S(1)}, f32[3,768]{1,0:T(4,128)}, u32[]{:S(2)}) copy-start(f32[3,768]{1,0:T(4,128)} %copy-done.3) | copy-start | bytes 27652 | tf_op jit(solution)/shard_map/while
  463.9 109.1 %all-gather.12.cloned.1.call-start = ((), (), s32[]{:S(2)}) async-start(), calls=%async_computation.4 | async-start | bytes 3158016 | tf_op jit(solution)/shard_map/while/body/eval_jaxpr/all_gather | solution.py:52
  467.1 0.6 copy-start.3
  467.8 108.5 %copy-start.4 = (f32[3,768]{1,0:T(4,128)S(1)}, f32[3,768]{1,0:T(4,128)}, u32[]{:S(2)}) copy-start(f32[3,768]{1,0:T(4,128)} %copy-done.3) | copy-start | bytes 27652 | tf_op jit(solution)/shard_map/while
  576.3 109.1 %all-gather.12.cloned.1.call-start = ((), (), s32[]{:S(2)}) async-start(), calls=%async_computation.4 | async-start | bytes 3158016 | tf_op jit(solution)/shard_map/while/body/eval_jaxpr/all_gather | solution.py:52
  579.6 0.6 copy-start.3
  580.2 108.5 %copy-start.4 = (f32[3,768]{1,0:T(4,128)S(1)}, f32[3,768]{1,0:T(4,128)}, u32[]{:S(2)}) copy-start(f32[3,768]{1,0:T(4,128)} %copy-done.3) | copy-start | bytes 27652 | tf_op jit(solution)/shard_map/while
  688.7 276.6 %all-reduce.8.cloned.1.call-start = ((), (), s32[]{:S(2)}) async-start(), calls=%async_computation.3 | async-start | bytes 393216
  697.4 2.6 copy-start.5
Sparse Core Ops, SparseCore 0:
  9.8 30.9 all-gather.7
  48.5 183.2 all-reduce.5
  236.1 104.0 all-gather.9
  356.3 104.2 all-gather.11
  468.7 104.2 all-gather.11
  581.1 104.2 all-gather.11
  714.5 177.2 all-reduce.7
where the time goes:
time: 975 us; the launch traced here: 974 us
  waiting for transfers between devices  637 us (65%)
  blocking collectives  251 us (26%)
  local copies, waits for them, and re-layouts  29.5 us (3%)
  matrix products  29.4 us (3%)
  between operations  16 us (2%)
  other arithmetic  10.7 us (1%)
    all_gather x4, waiting for transfers between devices, gather_spread(): return lax.all_gather(rows, ('dp', 'dim'), axis=0, tiled=True)  422 us
    unnamed x1, blocking collectives  251 us
    unnamed x6, waiting for transfers between devices  183 us
    all_gather x1, waiting for transfers between devices, per_device(): gathered_rows = lax.all_gather(vectors, 'dim', axis=0, tiled=True)  31.9 us
  transfers between devices with their start and end apart: 7, of which 6 were waited for; matrix products, arithmetic and copies ran while one was open for 0% of the time, Pallas kernels for 0%

commit v1 on v0

--- a/solution.py
+++ b/solution.py
@@ -49,7 +49,14 @@
     dim_index = lax.axis_index("dim")
 
     def gather_spread(rows):
-        return lax.all_gather(rows, ("dp", "dim"), axis=0, tiled=True)
+
+        def gates_plan(content, named_axis):
+            h_now = lax.psum(1, named_axis)
+            step_out = jnp.stack(h_now * [content], axis=0)
+            vec_out = lax.all_to_all(step_out, named_axis, split_axis=0, concat_axis=0)
+            return jnp.concatenate(vec_out, axis=0)
+
+        return gates_plan(rows, ("dp", "dim"))
 
     gathered = gather_spread(own_rows)
     magnitude = jnp.sqrt(jnp.sum(gathered * gathered))

time: 975 us -> 891 us (0.914)
  waiting for transfers between devices: 637 us -> 520 us
  starting transfers between devices: 0.28 us -> 34.5 us
    all_gather x4 -> x0, waiting for transfers between devices: 422 us -> none  [gather_spread(): return lax.all_gather(rows, ('dp', 'dim'), axis=0, tiled=True)]
    all_to_all x0 -> x4, waiting for transfers between devices: none -> 305 us  [gates_plan(): vec_out = lax.all_to_all(step_out, named_axis, split_axis=0, concat_axis=0)]
    all_to_all x0 -> x4, starting transfers between devices: none -> 34.3 us  [gates_plan(): vec_out = lax.all_to_all(step_out, named_axis, split_axis=0, concat_axis=0)]
    while x19 -> x4, local copies, waits for them, and re-layouts: 11.5 us -> 0.01 us
    unnamed x6 -> x5, waiting for transfers between devices: 183 us -> 183 us
where the time goes in v1:
time: 891 us; the launch traced here: 890 us
  waiting for transfers between devices  520 us (58%)
  blocking collectives  246 us (28%)
  local copies, waits for them, and re-layouts  35.4 us (4%)
  starting transfers between devices  34.5 us (4%)
  matrix products  29.4 us (3%)
  between operations  15.7 us (2%)
    all_to_all x4, waiting for transfers between devices, gates_plan(): vec_out = lax.all_to_all(step_out, named_axis, split_axis=0, concat_axis=0)  305 us
    unnamed x1, blocking collectives  246 us
    unnamed x5, waiting for transfers between devices  183 us
    all_to_all x4, starting transfers between devices, gates_plan(): vec_out = lax.all_to_all(step_out, named_axis, split_axis=0, concat_axis=0)  34.3 us
    all_gather x1, waiting for transfers between devices, per_device(): gathered_rows = lax.all_gather(vectors, 'dim', axis=0, tiled=True)  31.9 us
  transfers between devices with their start and end apart: 7, of which 6 were waited for; matrix products, arithmetic and copies ran while one was open for 0% of the time, Pallas kernels for 0%

profile of v1, /device:TPU:8, one launch (start us, length us, event | category | flops | bytes accessed | tf_op | source)
XLA Modules:
  0.0 889.7 jit_solution(16600456956071933018)
XLA Ops:
  7.2 0.7 all-gather.2.cloned.1.call-update
  8.0 0.9 reshape.46
  8.9 31.9 %all-gather.2.cloned.1.call-done = bf16[768,1024]{1,0:T(8,128)(2,1)} async-done(((bf16[192,1024]{1,0:T(8,128)(2,1)}), bf16[768,1024]{1,0:T(8,128)(2,1)}) %all-gather.2.cloned.1.call-update) | async-done | bytes 1572880 | tf_op jit(solution)/shard_map/all_gather | solution.py:22
  40.8 6.8 while.43
  40.8 0.8 constant_dynamic-slice_fusion.8
  41.5 2.0 fusion.57
  43.5 0.1 convert_element_type.62
  43.6 0.5 convolution_add_fusion.2
  44.2 0.8 constant_dynamic-slice_fusion.8
  44.9 2.0 fusion.57
  46.9 0.1 convert_element_type.62
  47.0 0.5 convolution_add_fusion.2
  47.6 0.8 copy-done.1
  48.4 0.6 dynamic-slice
  49.6 182.2 %all-reduce.6.cloned.1.call-done = f32[192,768]{1,0:T(8,128)} async-done(((f32[192,768]{1,0:T(8,128)}), f32[192,768]{1,0:T(8,128)}) %all-reduce.6.cloned.1.call-update) | async-done | bytes 589840
  231.8 0.8 constant_dynamic-slice_fusion.4
  232.6 2.1 stack.4
  234.7 10.5 %all-to-all-start.1 = ((f32[256,3,768]{2,1,0:T(4,128)}), f32[256,3,768]{2,1,0:T(4,128)S(1)}, u32[]{:S(2)}, u32[]{:S(2)}) async-start(f32[256,3,768]{2,1,0:T(4,128)} %stack.4), calls=%async_computation.1 | async-start | bytes 6291456 | tf_op jit(solution)/shard_map/all_to_all | solution.py:56
  245.1 0.0 all-reduce.8.cloned.1.call-start
  245.8 76.2 %all-to-all-done.1 = f32[256,3,768]{2,1,0:T(4,128)S(1)} async-done(((f32[256,3,768]{2,1,0:T(4,128)}), f32[256,3,768]{2,1,0:T(4,128)S(1)}, u32[]{:S(2)}, u32[]{:S(2)}) %all-to-all-start.1) | async-done | bytes 2359328 | tf_op jit(solution)/shard_map/all_to_all | solution.py:56
  322.0 2.2 multiply_reduce_fusion
  324.9 2.2 broadcast_divide_fusion
  327.1 3.2 div.22
  330.4 0.8 broadcast_divide_fusion.1
  331.2 278.2 %while.42 = (s32[]{:T(128)}, f32[3,768]{1,0:T(4,128)S(1)}, f32[768,768]{1,0:T(8,128)S(1)}, s32[]{:T(128)}) while((s32[]{:T(128)}, f32[3,768]{1,0:T(4,128)S(1)}, f32[768,768]{1,0:T(8,128)S(1)}, s32[]{:T(128)}) %tuple.81), condition=%wide.region_5.0_spmd, body=%wide.region_4.0_spmd.sunk | while | flops 42474240 | bytes 20502612 | solution.py:71
  331.2 2.0 fusion.52
  333.2 1.2 fusion.53
  334.4 2.1 stack.6
  336.5 8.0 all-to-all-start
  344.5 76.2 %all-to-all-done = f32[256,3,768]{2,1,0:T(4,128)} async-done(((f32[256,3,768]{2,1,0:T(4,128)}), f32[256,3,768]{2,1,0:T(4,128)}, u32[]{:S(2)}, u32[]{:S(2)}) %all-to-all-start) | async-done | bytes 2359328 | tf_op jit(solution)/shard_map/while/body/eval_jaxpr/all_to_all | solution.py:56
  420.6 3.2 reshape.61
  423.9 2.0 fusion.52
  425.9 1.2 fusion.53
  427.1 2.1 stack.6
  429.2 8.0 all-to-all-start
  437.2 76.2 %all-to-all-done = f32[256,3,768]{2,1,0:T(4,128)} async-done(((f32[256,3,768]{2,1,0:T(4,128)}), f32[256,3,768]{2,1,0:T(4,128)}, u32[]{:S(2)}, u32[]{:S(2)}) %all-to-all-start) | async-done | bytes 2359328 | tf_op jit(solution)/shard_map/while/body/eval_jaxpr/all_to_all | solution.py:56
  513.4 3.2 reshape.61
  516.6 2.0 fusion.52
  518.6 1.2 fusion.53
  519.9 2.1 stack.6
  522.0 8.0 all-to-all-start
  529.9 76.2 %all-to-all-done = f32[256,3,768]{2,1,0:T(4,128)} async-done(((f32[256,3,768]{2,1,0:T(4,128)}), f32[256,3,768]{2,1,0:T(4,128)}, u32[]{:S(2)}, u32[]{:S(2)}) %all-to-all-start) | async-done | bytes 2359328 | tf_op jit(solution)/shard_map/while/body/eval_jaxpr/all_to_all | solution.py:56
  606.1 3.2 reshape.61
  609.4 2.6 reshape.47
  611.9 2.1 constant_dynamic-slice_fusion.5
  614.1 1.4 reshape.48
  615.5 2.5 fusion.21
  618.0 2.6 fusion.19
  620.6 12.7 %while.44 = (s32[]{:T(128)}, f32[256,16,12]{0,2,1:T(8,128)}, f32[256,16]{0,1:T(8,128)S(1)}, bf16[768,1024]{1,0:T(8,128)(2,1)}, bf16[192,768]{1,0:T(8,128)(2,1)S(...) while((s32[]{:T(128)}, f32[256,16,12]{0,2,1:T(8,128)}, ...), condition=%wide.region_8.0_spmd.clone, body=%wide.region_6.0_spmd.clone.sunk | while | flops 212013056 | bytes 2457766 | solution.py:92
  620.6 1.5 convolution_convert_fusion.2
  622.1 2.8 fusion.61
  624.9 1.4 convert_reduce_fusion.2
  626.4 1.5 convolution_convert_fusion.2
  627.9 3.9 fusion.61
  631.9 1.4 convert_reduce_fusion.2
  633.3 1.6 reshape.49
  635.0 246.2 %all-reduce.2 = f32[256,16]{0,1:T(8,128)S(1)} all-reduce(f32[256,16]{0,1:T(8,128)S(1)} %get-tuple-element.256), channel_id=4, replica_groups=mesh['dp'=64,'dim'=4] {'dp'}, use_global_device_ids=true, to_apply=%region_10.0.clone | all-reduce | flops 4096 | bytes 32768
  881.1 0.1 constant_dynamic-slice_fusion.2
  881.2 0.1 copy.13
  881.3 0.1 broadcast_in_dim.27
  881.4 0.1 reshape.50
  881.5 1.0 constant_dynamic-slice_fusion.3
  882.5 0.1 copy.14
  882.6 0.6 div.23
  (24 shorter events, 0.3 us)
Async XLA Ops:
  7.2 33.6 %all-gather.2.cloned.1.call-start = ((), (), s32[]{:S(2)}) async-start(), calls=%async_computation.2 | async-start | bytes 1966080 | tf_op jit(solution)/shard_map/all_gather | solution.py:22
  7.9 223.9 %all-reduce.6.cloned.1.call-start = ((), (), s32[]{:S(2)}) async-start(), calls=%async_computation.3 | async-start | bytes 1179648
  40.8 7.6 copy-start.3
  41.5 2.1 copy-start
  44.9 2.1 copy-start
  47.5 0.8 copy-start.1
  234.7 87.4 %all-to-all-start.1 = ((f32[256,3,768]{2,1,0:T(4,128)}), f32[256,3,768]{2,1,0:T(4,128)S(1)}, u32[]{:S(2)}, u32[]{:S(2)}) async-start(f32[256,3,768]{2,1,0:T(4,128)} %stack.4), calls=%async_computation.1 | async-start | bytes 6291456 | tf_op jit(solution)/shard_map/all_to_all | solution.py:56
  245.1 636.4 %all-reduce.8.cloned.1.call-start = ((), (), s32[]{:S(2)}) async-start(), calls=%async_computation.4 | async-start | bytes 393216
  336.5 84.1 %all-to-all-start = ((f32[256,3,768]{2,1,0:T(4,128)}), f32[256,3,768]{2,1,0:T(4,128)}, u32[]{:S(2)}, u32[]{:S(2)}) async-start(f32[256,3,768]{2,1,0:T(4,128)} %stack.6), calls=%async_computation | async-start | bytes 6291456 | tf_op jit(solution)/shard_map/while/body/eval_jaxpr/all_to_all | solution.py:56
  429.2 84.1 %all-to-all-start = ((f32[256,3,768]{2,1,0:T(4,128)}), f32[256,3,768]{2,1,0:T(4,128)}, u32[]{:S(2)}, u32[]{:S(2)}) async-start(f32[256,3,768]{2,1,0:T(4,128)} %stack.6), calls=%async_computation | async-start | bytes 6291456 | tf_op jit(solution)/shard_map/while/body/eval_jaxpr/all_to_all | solution.py:56
  522.0 84.1 %all-to-all-start = ((f32[256,3,768]{2,1,0:T(4,128)}), f32[256,3,768]{2,1,0:T(4,128)}, u32[]{:S(2)}, u32[]{:S(2)}) async-start(f32[256,3,768]{2,1,0:T(4,128)} %stack.6), calls=%async_computation | async-start | bytes 6291456 | tf_op jit(solution)/shard_map/while/body/eval_jaxpr/all_to_all | solution.py:56
  618.0 2.6 copy-start.2
Sparse Core Ops, SparseCore 0:
  9.8 30.9 all-gather.1
  48.5 183.2 all-reduce.5
  635.1 171.8 all-reduce.7
